TPU v7x, 32 devices: a whole 2x2x4 slice. The times are simulated.
32 devices in a mesh: rows: 16 (over z, x, core), cols: 2 (over y).
Axes of the slice: x: 2, y: 2, z: 4, core: 2. Of those that a mesh axis runs over, the one named last changes fastest.
Arguments:
- kernel: float32 [16384, 1536], P('rows', 'cols'), may hold values from -0.15625 to 0.15625
- row_orbitals: float32 [16384, 512], P('rows', 'cols'), may hold values from -1.5 to 1.5
- col_orbitals: float32 [1536, 512], P('cols', 'rows'), may hold values from -1.5 to 1.5
- col_vectors: float32 [1536, 512], P('cols', 'rows'), may hold values from -6 to 6
Outputs:
- exchange: float32 [512, 16384], P('cols', 'rows')
All inputs are finite; a program needn't handle non-finite values.
Results may differ from a plain program's by a relative error of at most 0.0003.
Values sent between devices are 32-bit elements; how exact they have to be, the bound alone decides.
A program may use at most 64 MiB of HBM per device.

v0:
```python
import jax
import jax.numpy as jnp
from jax import lax
from jax.sharding import PartitionSpec as P


def body(kernel, row_orbitals, col_orbitals, col_vectors):
    full_rows = lax.all_gather(row_orbitals, "cols", axis=1, tiled=True)
    full_cols = lax.all_gather(col_orbitals, "rows", axis=1, tiled=True)
    full_vecs = lax.all_gather(col_vectors, "rows", axis=1, tiled=True)
    gram = jnp.dot(
        full_rows, full_cols.T, precision=lax.Precision.HIGHEST, preferred_element_type=jnp.float32
    )
    weighted = kernel * gram
    return lax.psum_scatter(
        -jnp.dot(
            full_vecs.T,
            weighted.T,
            precision=lax.Precision.HIGHEST,
            preferred_element_type=jnp.float32,
        ),
        "cols",
        scatter_dimension=0,
        tiled=True,
    )


def solution(mesh):
    in_specs = (P("rows", "cols"), P("rows", "cols"), P("cols", "rows"), P("cols", "rows"))
    out_specs = P("cols", "rows")
    return jax.shard_map(body, mesh=mesh, in_specs=in_specs, out_specs=out_specs, check_vma=False)
```

profile of v0, /device:TPU:0, one launch (start us, length us, event | category | flops | bytes accessed | tf_op | source)
XLA Modules:
  0.0 175.4 jit_solution(11052527146017626073)
XLA Ops:
  6.5 0.0 all-gather.4.cloned.1.call-start
  6.5 0.7 all-gather.4.cloned.1.call-update
  7.3 0.0 all-gather.6.cloned.1.call-start
  7.3 0.7 all-gather.6.cloned.1.call-update
  8.0 0.0 all-gather.8.cloned.1.call-start
  8.1 0.7 all-gather.8.cloned.1.call-update
  8.7 0.0 reduce-scatter.2.cloned.1.call-start
  8.8 35.9 %all-gather.4.cloned.1.call-done = f32[1024,512]{1,0:T(8,128)} async-done(((f32[1024,256]{1,0:T(8,128)}), f32[1024,512]{1,0:T(8,128)}) %all-gather.4.cloned.1.call-update) | async-done | bytes 2097168 | tf_op jit(solution)/shard_map/all_gather | solution.py:8
  44.7 41.9 %all-gather.6.cloned.1.call-done = f32[768,512]{0,1:T(8,128)} async-done(((f32[768,32]{0,1:T(8,128)}), f32[768,512]{0,1:T(8,128)}) %all-gather.6.cloned.1.call-update) | async-done | bytes 1572880 | tf_op jit(solution)/shard_map/all_gather | solution.py:9
  86.6 7.2 %fusion.4 = f32[1024,768]{1,0:T(8,128)S(1)} fusion(f32[1024,512]{1,0:T(8,128)} %all-gather.4.cloned.1.call-done, f32[768,512]{0,1:T(8,128)} %all-gather.6.cloned.1.call-done), kind=kOutput, calls=%fused_computation.3 | convolution fusion | flops 4831838208 | bytes 6815744 | tf_op jit(solution)/shard_map/dot_general | solution.py:11
  93.9 33.4 %all-gather.8.cloned.1.call-done = f32[768,512]{0,1:T(8,128)} async-done(((f32[768,32]{0,1:T(8,128)}), f32[768,512]{0,1:T(8,128)}) %all-gather.8.cloned.1.call-update) | async-done | bytes 1572880 | tf_op jit(solution)/shard_map/all_gather | solution.py:10
  127.3 8.3 %negate_bitcast_fusion = f32[512,1024]{0,1:T(8,128)} fusion(f32[768,512]{0,1:T(8,128)} %all-gather.8.cloned.1.call-done, f32[1024,768]{1,0:T(8,128)} %param.4, f32[1024,768]{1,0:T(8,128)S(1)} %fusion.4), kind=kOutput, calls=%fused_computation.2 | convolution fusion | flops 4833148928 | bytes 9961472 | tf_op jit(solution)/shard_map/dot_general | solution.py:16
  135.6 0.0 reduce-scatter.2.cloned.1.call-update
  135.6 30.8 %reduce-scatter.2.cloned.1.call-done = f32[256,1024]{0,1:T(8,128)} async-done(((f32[512,1024]{0,1:T(8,128)}), f32[256,1024]{0,1:T(8,128)}) %reduce-scatter.2.cloned.1.call-update) | async-done | bytes 1048592 | tf_op jit(solution)/shard_map/reduce_scatter | solution.py:15
  166.4 2.5 %copy.5 = f32[256,1024]{1,0:T(8,128)} copy(f32[256,1024]{0,1:T(8,128)} %reduce-scatter.2.cloned.1.call-done) | data formatting | bytes 2097152 | tf_op jit(solution)/shard_map/reduce_scatter | solution.py:15
Async XLA Ops:
  6.5 38.2 %all-gather.4.cloned.1.call-start = ((), (), s32[]{:S(2)}) async-start(), calls=%async_computation.1 | async-start | bytes 3145728 | tf_op jit(solution)/shard_map/all_gather | solution.py:8
  7.3 79.4 %all-gather.6.cloned.1.call-start = ((), (), s32[]{:S(2)}) async-start(), calls=%async_computation.2 | async-start | bytes 1671168 | tf_op jit(solution)/shard_map/all_gather | solution.py:9
  8.0 119.3 %all-gather.8.cloned.1.call-start = ((), (), s32[]{:S(2)}) async-start(), calls=%async_computation.3 | async-start | bytes 1671168 | tf_op jit(solution)/shard_map/all_gather | solution.py:10
  8.7 157.6 %reduce-scatter.2.cloned.1.call-start = ((), (), s32[]{:S(2)}) async-start(), calls=%async_computation.4 | async-start | bytes 3145728 | tf_op jit(solution)/shard_map/reduce_scatter | solution.py:15
Sparse Core Ops, SparseCore 0:
  8.9 35.8 all-gather.3
  47.0 39.5 all-gather.5
  88.9 38.2 all-gather.7
  135.7 30.6 reduce-scatter.1
where the time goes:
time: 176 us; the launch traced here: 175 us
  waiting for transfers between devices  144 us (82%)
  matrix products  15.6 us (9%)
  between operations  13.1 us (7%)
  local copies, waits for them, and re-layouts  2.53 us (1%)
    all_gather x1, waiting for transfers between devices, body(): full_cols = lax.all_gather(col_orbitals, 'rows', axis=1, tiled=True)  41.9 us
    all_gather x1, waiting for transfers between devices, body(): full_rows = lax.all_gather(row_orbitals, 'cols', axis=1, tiled=True)  35.9 us
    all_gather x1, waiting for transfers between devices, body(): full_vecs = lax.all_gather(col_vectors, 'rows', axis=1, tiled=True)  33.4 us
    reduce_scatter x1, waiting for transfers between devices, body(): lax.psum_scatter(-jnp.dot(full_vecs.T, weighted.T, precision=lax.Precisio...  30.8 us
    dot_general x1, matrix products, body(): jnp.dot(full_vecs.T, weighted.T, precision=lax.Precision.HIGHEST, preferr...  8.31 us
    dot_general x1, matrix products, body(): jnp.dot(full_rows, full_cols.T, precision=lax.Precision.HIGHEST, preferre...  7.25 us
  transfers between devices with their start and end apart: 4, of which 4 were waited for; matrix products, arithmetic and copies ran while one was open for 4% of the time, Pallas kernels for 0%

commit v1 on v0

--- a/solution.py
+++ b/solution.py
@@ -1,13 +1,22 @@
+import functools
 import jax
 import jax.numpy as jnp
 from jax import lax
 from jax.sharding import PartitionSpec as P
 
 
+def _try_all_vector(matrix, mesh_dim):
+    outcome_arr = jnp.concatenate(lax.all_gather(matrix, mesh_dim), 1)
+    return outcome_arr
+
+
+_pass_figure = functools.partial(_try_all_vector, mesh_dim="rows")
+
+
 def body(kernel, row_orbitals, col_orbitals, col_vectors):
     full_rows = lax.all_gather(row_orbitals, "cols", axis=1, tiled=True)
     full_cols = lax.all_gather(col_orbitals, "rows", axis=1, tiled=True)
-    full_vecs = lax.all_gather(col_vectors, "rows", axis=1, tiled=True)
+    full_vecs = _pass_figure(col_vectors)
     gram = jnp.dot(
         full_rows, full_cols.T, precision=lax.Precision.HIGHEST, preferred_element_type=jnp.float32
     )

time: 176 us -> 182 us (1.034)
  waiting for transfers between devices: 144 us -> 149 us
  local copies, waits for them, and re-layouts: 2.53 us -> 5.34 us
    all_gather x1, waiting for transfers between devices: 33.4 us -> 43.2 us  [_try_all_vector(): outcome_arr = jnp.concatenate(lax.all_gather(matrix, mesh_dim), 1)]
    all_gather x1, waiting for transfers between devices: 35.9 us -> 30.6 us  [body(): full_rows = lax.all_gather(row_orbitals, 'cols', axis=1, tiled=True)]
    unnamed x0 -> x3, local copies, waits for them, and re-layouts: none -> 1.89 us
    dot_general x1, matrix products: 8.31 us -> 6.46 us  [body(): jnp.dot(full_vecs.T, weighted.T, precision=lax.Precision.HIGHEST, preferr...]
  transfers between devices with their start and end apart: 4 -> 4, of which waited for: 4 -> 4; matrix products, arithmetic and copies ran while one was open for 4% -> 2% of each run, Pallas kernels for 0% -> 0%
where the time goes in v1:
time: 182 us; the launch traced here: 181 us
  waiting for transfers between devices  149 us (82%)
  matrix products  14.2 us (8%)
  between operations  13.2 us (7%)
  local copies, waits for them, and re-layouts  5.34 us (3%)
    all_gather x1, waiting for transfers between devices, _try_all_vector(): outcome_arr = jnp.concatenate(lax.all_gather(matrix, mesh_dim), 1)  43.2 us
    all_gather x1, waiting for transfers between devices, body(): full_cols = lax.all_gather(col_orbitals, 'rows', axis=1, tiled=True)  41.9 us
    reduce_scatter x1, waiting for transfers between devices, body(): lax.psum_scatter(-jnp.dot(full_vecs.T, weighted.T, precision=lax.Precisio...  30.8 us
    all_gather x1, waiting for transfers between devices, body(): full_rows = lax.all_gather(row_orbitals, 'cols', axis=1, tiled=True)  30.6 us
    dot_general x1, matrix products, body(): jnp.dot(full_rows, full_cols.T, precision=lax.Precision.HIGHEST, preferre...  7.69 us
    dot_general x1, matrix products, body(): jnp.dot(full_vecs.T, weighted.T, precision=lax.Precision.HIGHEST, preferr...  6.46 us
  transfers between devices with their start and end apart: 4, of which 4 were waited for; matrix products, arithmetic and copies ran while one was open for 2% of the time, Pallas kernels for 0%

profile of v1, /device:TPU:0, one launch (start us, length us, event | category | flops | bytes accessed | tf_op | source)
XLA Modules:
  0.0 181.3 jit_solution(101588713476415849)
XLA Ops:
  6.5 0.0 all-gather.9.cloned.1.call-start
  6.5 0.7 all-gather.9.cloned.1.call-update
  7.3 0.0 all-gather.5.cloned.1.call-start
  7.3 0.7 all-gather.5.cloned.1.call-update
  8.0 0.0 all-gather.7.cloned.1.call-start
  8.1 0.7 all-gather.7.cloned.1.call-update
  8.7 0.0 reduce-scatter.2.cloned.1.call-start
  8.8 43.2 %all-gather.9.cloned.1.call-done = f32[12288,32]{0,1:T(8,128)} async-done(((f32[768,32]{0,1:T(8,128)}), f32[12288,32]{0,1:T(8,128)}) %all-gather.9.cloned.1.call-update) | async-done | bytes 1572880 | tf_op jit(solution)/shard_map/all_gather | solution.py:9
  52.0 1.9 %copy.9 = f32[4,8,16,768]{3,2,1,0:T(8,128)S(1)} copy(f32[4,8,16,768]{3,1,2,0:T(8,128)} %bitcast.14) | data formatting | bytes 3145728
  53.9 0.9 copy.7
  54.8 30.6 %all-gather.5.cloned.1.call-done = f32[1024,512]{1,0:T(8,128)} async-done(((f32[1024,256]{1,0:T(8,128)}), f32[1024,512]{1,0:T(8,128)}) %all-gather.5.cloned.1.call-update) | async-done | bytes 2097168 | tf_op jit(solution)/shard_map/all_gather | solution.py:17
  85.4 41.9 %all-gather.7.cloned.1.call-done = f32[768,512]{0,1:T(8,128)} async-done(((f32[768,32]{0,1:T(8,128)}), f32[768,512]{0,1:T(8,128)}) %all-gather.7.cloned.1.call-update) | async-done | bytes 1572880 | tf_op jit(solution)/shard_map/all_gather | solution.py:18
  127.3 0.0 copy-start
  127.3 7.7 %fusion.4 = f32[1024,768]{1,0:T(8,128)S(1)} fusion(f32[1024,512]{1,0:T(8,128)} %all-gather.5.cloned.1.call-done, f32[768,512]{0,1:T(8,128)} %all-gather.7.cloned.1.call-done), kind=kOutput, calls=%fused_computation.3 | convolution fusion | flops 4831838208 | bytes 6815744 | tf_op jit(solution)/shard_map/dot_general | solution.py:20
  135.0 0.0 copy-done
  135.0 6.5 %negate_bitcast_fusion = f32[512,1024]{0,1:T(8,128)} fusion(f32[768,512]{0,1:T(8,128)S(1)} %bitcast.12, f32[1024,768]{1,0:T(8,128)S(1)} %copy-done, f32[1024,768]{1,0:T(8,128)S(1)} %fusion.4), kind=kOutput, calls=%fused_computation.2 | convolution fusion | flops 4833148928 | bytes 9961472 | tf_op jit(solution)/shard_map/dot_general | solution.py:25
  141.5 0.0 reduce-scatter.2.cloned.1.call-update
  141.5 30.8 %reduce-scatter.2.cloned.1.call-done = f32[256,1024]{0,1:T(8,128)} async-done(((f32[512,1024]{0,1:T(8,128)}), f32[256,1024]{0,1:T(8,128)}) %reduce-scatter.2.cloned.1.call-update) | async-done | bytes 1048592 | tf_op jit(solution)/shard_map/reduce_scatter | solution.py:24
  172.3 2.5 %copy.8 = f32[256,1024]{1,0:T(8,128)} copy(f32[256,1024]{0,1:T(8,128)} %reduce-scatter.2.cloned.1.call-done) | data formatting | bytes 2097152 | tf_op jit(solution)/shard_map/reduce_scatter | solution.py:24
Async XLA Ops:
  6.5 45.5 %all-gather.9.cloned.1.call-start = ((), (), s32[]{:S(2)}) async-start(), calls=%async_computation.4 | async-start | bytes 1671168 | tf_op jit(solution)/shard_map/all_gather | solution.py:9
  7.3 78.1 %all-gather.5.cloned.1.call-start = ((), (), s32[]{:S(2)}) async-start(), calls=%async_computation.1 | async-start | bytes 3145728 | tf_op jit(solution)/shard_map/all_gather | solution.py:17
  8.0 119.3 %all-gather.7.cloned.1.call-start = ((), (), s32[]{:S(2)}) async-start(), calls=%async_computation.2 | async-start | bytes 1671168 | tf_op jit(solution)/shard_map/all_gather | solution.py:18
  8.7 163.5 %reduce-scatter.2.cloned.1.call-start = ((), (), s32[]{:S(2)}) async-start(), calls=%async_computation.3 | async-start | bytes 3145728 | tf_op jit(solution)/shard_map/reduce_scatter | solution.py:24
  127.3 7.7 %copy-start = (f32[1024,768]{1,0:T(8,128)S(1)}, f32[1024,768]{1,0:T(8,128)}, u32[]{:S(2)}) copy-start(f32[1024,768]{1,0:T(8,128)} %param.4) | copy-start | bytes 9437188
Sparse Core Ops, SparseCore 0:
  9.6 42.3 all-gather.8
  53.5 31.8 all-gather.4
  87.7 39.5 all-gather.6
  141.6 30.6 reduce-scatter.1
